TPU v7x, 1024 devices: a whole 8x8x8 slice. The times are simulated.
1024 devices in a mesh: row: 16 (over x, z_lo), col: 64 (over y, z_hi, core).
Axes of the slice: x: 8, y: 8, z: 8 (z_hi: 4, z_lo: 2; z = z_hi * 2 + z_lo), core: 2. Of those that a mesh axis runs over, the one named last changes fastest.
Arguments:
- tokens: bfloat16 [256, 10240], P('col', 'row'), may hold values from -6 to 6
- out_grad: bfloat16 [256, 10240], P('col', 'row'), may hold values from -3 to 3
- gate_weight: bfloat16 [10240, 26624], P('row', 'col'), may hold values from -0.0625 to 0.0625
- up_weight: bfloat16 [10240, 26624], P('row', 'col'), may hold values from -0.0625 to 0.0625
- down_weight: bfloat16 [26624, 10240], P('col', 'row'), may hold values from -0.0390625 to 0.0390625
- gate_mask: int32 [2560, 6656], P('row', 'col'), may hold values from 0 to 23
- up_mask: int32 [2560, 6656], P('row', 'col'), may hold values from 0 to 23
- down_mask: int32 [6656, 2560], P('col', 'row'), may hold values from 0 to 23
Outputs:
- input_grad: bfloat16 [256, 10240], P('col', 'row')
- gate_weight_grad: bfloat16 [10240, 26624], P('row', 'col')
- up_weight_grad: bfloat16 [10240, 26624], P('row', 'col')
- down_weight_grad: bfloat16 [26624, 10240], P('col', 'row')
Inputs may be any that keep to these rules, and one draw needn't show every extreme that they name: `gate_mask`: each entry is a pattern code as the first step defines, so every row and every column of each 4 by 4 block of a pruned weight keeps exactly two entries. `up_mask`: as for gate_mask. `down_mask`: as for gate_mask.
All inputs are finite; a program needn't handle non-finite values.
Results may differ from a plain program's by a relative error of at most 0.0049.
Values may be sent and summed in bfloat16 or wider, within the bound.
A program may use at most 32 MiB of HBM per device.

v0:
```python
import jax
import jax.numpy as jnp
from jax import lax
from jax.sharding import PartitionSpec as P


def sent_together(arrays, axis, dim, along):
    ends, at = ([], 0)
    for a in arrays[:-1]:
        at += a.shape[along]
        ends.append(at)
    both = jnp.concatenate(arrays, axis=along)
    return tuple(jnp.split(lax.all_gather(both, axis, axis=dim, tiled=True), ends, axis=along))


def in_blocks(array, dim, size):
    before, after = (array.shape[:dim], array.shape[dim + 1 :])
    return jnp.moveaxis(array.reshape(*before, size, -1, *after), dim, 0)


def summed_on_arrival(array, axis, dim):
    pieces = in_blocks(array, dim, lax.axis_size(axis))
    arrived = lax.all_to_all(pieces, axis, split_axis=0, concat_axis=0, tiled=True)
    return arrived.sum(axis=0)


def in_order(pieces, dim):
    lengths = list(pieces.shape[1:])
    lengths[dim] *= pieces.shape[0]
    return jnp.moveaxis(pieces, 0, dim).reshape(lengths)


def sent_to_all(array, axis):
    size = lax.axis_size(axis)
    return lax.all_to_all(
        jnp.broadcast_to(array[None], (size, *array.shape)), axis, 0, 0, tiled=True
    )


def gathered_copies(array, axis, dim):
    return in_order(sent_to_all(array, axis), dim)


def expand_mask(block_ids):
    lead_col = block_ids // 6
    second_rank = block_ids // 2 % 3
    third_rank = block_ids % 2
    second_col = second_rank + (second_rank >= lead_col).astype(jnp.int32)
    low_col = jnp.minimum(lead_col, second_col)
    high_col = jnp.maximum(lead_col, second_col)
    rest_low = jnp.where(low_col > 0, 0, jnp.where(high_col > 1, 1, 2)).astype(jnp.int32)
    rest_high = 6 - low_col - high_col - rest_low
    third_col = jnp.where(third_rank == 0, rest_low, rest_high)
    fourth_col = 6 - lead_col - second_col - third_col
    ordering = [lead_col, second_col, third_col, fourth_col]
    group_rows, group_cols = block_ids.shape
    col_position = lax.broadcasted_iota(jnp.int32, (group_rows, 4 * group_cols), 1) % 4
    row_list = []
    for local_row in range(4):
        current = jnp.repeat(ordering[local_row], 4, axis=1)
        following = jnp.repeat(ordering[(local_row + 1) % 4], 4, axis=1)
        row_list.append((current == col_position) | (following == col_position))
    pattern = jnp.stack(row_list, axis=1).reshape(4 * group_rows, 4 * group_cols)
    return pattern.astype(jnp.bfloat16)


def contract_last(left, right):
    return lax.dot_general(
        left, right, (((1,), (1,)), ((), ())), preferred_element_type=jnp.float32
    )


def contract_first(left, right):
    return lax.dot_general(
        left, right, (((0,), (0,)), ((), ())), preferred_element_type=jnp.float32
    )


def local(tokens, out_grad, gate_weight, up_weight, down_weight, gate_mask, up_mask, down_mask):
    gate_keep = expand_mask(gate_mask)
    up_keep = expand_mask(up_mask)
    down_keep = expand_mask(down_mask)
    gate_pruned = gate_weight * gate_keep
    up_pruned = up_weight * up_keep
    down_pruned = down_weight * down_keep
    panel_width = gate_pruned.shape[1]
    all_tokens, all_grads = sent_together((tokens, out_grad), "col", 0, 1)
    gate_sum = jnp.dot(all_tokens, gate_pruned, preferred_element_type=jnp.float32)
    up_sum = jnp.dot(all_tokens, up_pruned, preferred_element_type=jnp.float32)
    back_sum = contract_last(all_grads, down_pruned)
    shares = summed_on_arrival(jnp.concatenate([gate_sum, up_sum, back_sum], axis=1), "row", 0)
    gate_sum = shares[:, :panel_width]
    up_sum = shares[:, panel_width : 2 * panel_width]
    back_sum = shares[:, 2 * panel_width :]
    logistic = jax.nn.sigmoid(gate_sum)
    swish_val = gate_sum * logistic
    hidden = swish_val * up_sum
    swiglu_up_grad = back_sum * swish_val
    swiglu_gate_grad = back_sum * up_sum * logistic * (1.0 + gate_sum * (1.0 - logistic))
    local_grads = jnp.concatenate([swiglu_gate_grad, swiglu_up_grad, hidden], axis=1).astype(
        jnp.bfloat16
    )
    all_local = gathered_copies(local_grads, "row", 0)
    gate_grad = all_local[:, :panel_width]
    up_grad = all_local[:, panel_width : 2 * panel_width]
    hidden = all_local[:, 2 * panel_width :]
    input_grad = summed_on_arrival(
        contract_last(gate_grad, gate_pruned) + contract_last(up_grad, up_pruned), "col", 0
    ).astype(jnp.bfloat16)
    gate_weight_grad = (contract_first(all_tokens, gate_grad) * gate_keep).astype(jnp.bfloat16)
    up_weight_grad = (contract_first(all_tokens, up_grad) * up_keep).astype(jnp.bfloat16)
    down_weight_grad = (contract_first(hidden, all_grads) * down_keep).astype(jnp.bfloat16)
    return (input_grad, gate_weight_grad, up_weight_grad, down_weight_grad)


def solution(mesh):
    in_specs = (
        P("col", "row"),
        P("col", "row"),
        P("row", "col"),
        P("row", "col"),
        P("col", "row"),
        P("row", "col"),
        P("row", "col"),
        P("col", "row"),
    )
    out_specs = (P("col", "row"), P("row", "col"), P("row", "col"), P("col", "row"))
    return jax.shard_map(local, mesh=mesh, in_specs=in_specs, out_specs=out_specs, check_vma=False)
```

profile of v0, /device:TPU:1, one launch (start us, length us, event | category | flops | bytes accessed | tf_op | source)
XLA Modules:
  0.0 214.6 jit_solution(2509657084103265741)
XLA Ops:
  0.7 1.1 subtract_select_fusion.1
  1.8 1.0 subtract_subtract_fusion.1
  2.8 0.1 copy.47
  2.9 1.1 subtract_select_fusion.2
  4.0 0.1 subtract_subtract_fusion.2
  4.1 0.1 copy.41
  4.2 0.1 copy.46
  4.3 0.1 broadcast_in_dim.73
  4.4 0.1 reshape.935
  4.7 0.1 reshape.936
  4.8 0.1 copy.40
  5.0 0.1 reshape.930
  5.2 0.1 reshape.931
  5.4 0.1 copy.48
  5.6 0.1 reshape.937
  5.7 0.1 copy.49
  5.9 0.1 reshape.938
  6.1 0.1 copy.42
  6.2 0.1 reshape.932
  6.4 0.3 fusion.50
  6.6 0.4 fusion.51
  7.0 0.3 fusion.52
  7.4 0.2 pad_add_fusion.1
  7.6 1.0 copy.50
  8.6 0.4 reshape.939
  9.1 97.6 %all-gather = bf16[64,4,1280]{2,1,0:T(4,128)(2,1)S(1)} all-gather(bf16[1,4,1280]{2,1,0:T(4,128)(2,1)S(1)} %maximum_bitcast_fusion), channel_id=1, replica_groups=mesh['row'=16,'col'=64] {'col'}, dimensions={0}, use_global_device_ids=true | all-gather | bytes 665600 | tf_op jit(solution)/shard_map/all_gather | solution.py:13
  106.6 0.2 reshape.949
  106.8 0.2 copy.51
  107.1 0.1 copy.43
  107.3 0.1 reshape.933
  107.4 0.2 fusion.55
  107.8 0.2 pad_add_fusion
  107.9 1.0 copy.44
  108.9 0.4 reshape.934
  109.3 0.2 copy.45
  109.6 0.2 copy-done.6
  109.8 0.2 subtract_select_fusion
  110.0 0.1 subtract_subtract_fusion
  110.4 0.3 fusion.8
  110.8 0.2 pad_add_fusion.2
  110.9 1.0 copy.52
  111.9 0.2 reshape.944
  112.1 0.5 fusion.11
  112.6 0.5 fusion.10
  113.1 0.6 copy-done.4
  113.6 0.4 fusion.3
  114.0 1.1 pad_maximum_fusion
  115.2 1.7 copy.53
  116.9 42.0 %all_to_all.15 = f32[16,16,1248]{2,1,0:T(8,128)} all-to-all(f32[16,16,1248]{2,1,0:T(8,128)S(1)} %bitcast.46), channel_id=1, replica_groups=mesh['row'=16,'col'=64] {'row'}, dimensions={0} | all-to-all | bytes 2555904 | tf_op jit(solution)/shard_map/all_to_all | solution.py:23
  158.9 1.4 reduce_sum.18
  160.2 0.1 multiply_convert_fusion
  160.3 0.1 concatenate.16
  160.5 23.0 %all_to_all.16 = bf16[16,16,1248]{2,1,0:T(8,128)(2,1)S(1)} all-to-all(bf16[16,16,1248]{2,1,0:T(8,128)(2,1)S(1)} %broadcast_in_dim.81), channel_id=1, replica_groups=mesh['row'=16,'col'=64] {'row'}, dimensions={0} | all-to-all | bytes 1277952 | tf_op jit(solution)/shard_map/all_to_all | solution.py:35
  183.5 0.4 fusion.9
  183.9 0.5 convolution_add_fusion
  184.4 1.0 reshape.947
  185.4 6.7 %all-to-all-start.2 = ((f32[64,4,640]{2,1,0:T(4,128)}), f32[64,4,640]{2,1,0:T(4,128)S(1)}, u32[]{:S(2)}, u32[]{:S(2)}) async-start(f32[64,4,640]{2,1,0:T(4,128)} %reshape.947), calls=%async_computation.2 | async-start | bytes 1310720 | tf_op jit(solution)/shard_map/all_to_all | solution.py:23
  192.1 0.4 copy.55
  192.5 0.4 copy.54
  192.9 1.3 fusion.2
  194.2 1.4 fusion.1
  195.6 1.2 fusion
  196.7 17.1 %all-to-all-done.2 = f32[64,4,640]{2,1,0:T(4,128)S(1)} async-done(((f32[64,4,640]{2,1,0:T(4,128)}), f32[64,4,640]{2,1,0:T(4,128)S(1)}, u32[]{:S(2)}, u32[]{:S(2)}) %all-to-all-start.2) | async-done | bytes 655392 | tf_op jit(solution)/shard_map/all_to_all | solution.py:23
  213.8 0.7 reduce_sum.19
  (35 shorter events, 1.0 us)
Async XLA Ops:
  0.6 3.4 %copy-start.5 = (s32[160,104]{1,0:T(8,128)S(1)}, s32[160,104]{1,0:T(8,128)}, u32[]{:S(2)}) copy-start(s32[160,104]{1,0:T(8,128)} %param.13) | copy-start | bytes 199684
  7.4 1.6 copy-start.7
  7.4 1.6 copy-start.8
  9.0 97.8 %copy-start.2 = (bf16[640,416]{0,1:T(8,128)(2,1)S(1)}, bf16[640,416]{0,1:T(8,128)(2,1)}, u32[]{:S(2)}) copy-start(bf16[640,416]{0,1:T(8,128)(2,1)} %param.11) | copy-start | bytes 1597444
  106.8 6.3 %copy-start = (bf16[256,1280]{1,0:T(8,128)(2,1)}, bf16[256,1280]{1,0:T(8,128)(2,1)S(1)}, u32[]{:S(2)}) copy-start(bf16[256,1280]{1,0:T(8,128)(2,1)S(1)} %reshape.949) | copy-start | bytes 1966084
  107.7 1.6 copy-start.3
  108.9 0.9 copy-start.6
  112.6 1.0 copy-start.4
  185.4 7.5 %copy-start.1 = (bf16[256,1280]{1,0:T(8,128)(2,1)S(1)}, bf16[256,1280]{1,0:T(8,128)(2,1)}, u32[]{:S(2)}) copy-start(bf16[256,1280]{1,0:T(8,128)(2,1)} %copy-done) | copy-start | bytes 1966084
  185.4 28.4 %all-to-all-start.2 = ((f32[64,4,640]{2,1,0:T(4,128)}), f32[64,4,640]{2,1,0:T(4,128)S(1)}, u32[]{:S(2)}, u32[]{:S(2)}) async-start(f32[64,4,640]{2,1,0:T(4,128)} %reshape.947), calls=%async_computation.2 | async-start | bytes 1310720 | tf_op jit(solution)/shard_map/all_to_all | solution.py:23
where the time goes:
time: 215 us
  blocking collectives  163 us (76%)
  waiting for transfers between devices  17.1 us (8%)
  local copies, waits for them, and re-layouts  11.8 us (5%)
  other arithmetic  9.24 us (4%)
  starting transfers between devices  6.66 us (3%)
  matrix products  6 us (3%)
    all_gather x1, blocking collectives, sent_together(): lax.all_gather(both, axis, axis=dim, tiled=True)  97.6 us
    all_to_all x1, blocking collectives, summed_on_arrival(): lax.all_to_all(pieces, axis, split_axis=0, concat_axis=0, tiled=True)  42 us
    all_to_all x1, blocking collectives, sent_to_all(): lax.all_to_all(jnp.broadcast_to(array[None], (size, *array.shape)), axis,...  23 us
    all_to_all x1, waiting for transfers between devices, summed_on_arrival(): lax.all_to_all(pieces, axis, split_axis=0, concat_axis=0, tiled=True)  17.1 us
    all_to_all x1, starting transfers between devices, summed_on_arrival(): lax.all_to_all(pieces, axis, split_axis=0, concat_axis=0, tiled=True)  6.66 us
  transfers between devices with their start and end apart: 1, of which 1 were waited for; matrix products, arithmetic and copies ran while one was open for 2% of the time, Pallas kernels for 0%

commit v1 on v0

v1 whole, which is shorter than its diff:
```python
import functools

import jax
import jax.numpy as jnp
from jax import lax
from jax.experimental import pallas as pl
from jax.experimental.pallas import tpu as pltpu
from jax.sharding import PartitionSpec as P

F32 = jnp.float32
BF16 = jnp.bfloat16
MESH = pl.DeviceIdType.MESH
TILE = 16


def dot(left, right, at):
    return lax.dot_general(
        left, right, (((at[0],), (at[1],)), ((), ())), preferred_element_type=F32
    )


def orderings(code):
    def step(value, bound):
        return (value >= bound).astype(jnp.int32)

    p0 = step(code, 6) + step(code, 12) + step(code, 18)
    rest = code - 6 * p0
    rank1 = step(rest, 2) + step(rest, 4)
    rank2 = rest - 2 * rank1
    p1 = rank1 + (rank1 >= p0).astype(jnp.int32)
    low, high = jnp.minimum(p0, p1), jnp.maximum(p0, p1)
    rest_low = jnp.where(low > 0, 0, jnp.where(high > 1, 1, 2))
    rest_high = 6 - low - high - rest_low
    p2 = jnp.where(rank2 == 0, rest_low, rest_high)
    return p0, p1, p2, 6 - p0 - p1 - p2


def nibbles(code, bits_are_columns):
    p = orderings(code)
    one = jnp.ones_like(code)
    kept = []
    for at in range(4):
        if bits_are_columns:
            kept.append((one << p[at]) | (one << p[(at + 1) % 4]))
        else:
            bits = jnp.zeros_like(code)
            for i in range(4):
                hit = (p[i] == at) | (p[(i + 1) % 4] == at)
                bits = bits | jnp.where(hit, 1 << i, 0)
            kept.append(bits)
    return [k.astype(F32).astype(BF16) for k in kept]


def expanded(code, bits_are_columns, width, height):
    quarter = width // 4
    parts = nibbles(code, bits_are_columns)
    wide = jnp.zeros((code.shape[1], width), F32)
    d = lax.broadcasted_iota(jnp.int32, (quarter, width), 1)
    a = lax.broadcasted_iota(jnp.int32, (quarter, width), 0)
    for i in range(4):
        spread = (d == 4 * a + i).astype(F32).astype(BF16)
        wide = wide + dot(parts[i], spread, (0, 0))
    f = lax.broadcasted_iota(jnp.int32, (height, height // 4), 0)
    b = lax.broadcasted_iota(jnp.int32, (height, height // 4), 1)
    tall = dot(((f >> 2) == b).astype(F32).astype(BF16), wide.astype(BF16), (1, 0))
    local = lax.broadcasted_iota(jnp.int32, (height, width), 0) & 3
    return ((tall.astype(jnp.int32) >> local) & 1).astype(F32)


def kernel(
    dims,
    tok, og, gw, uw, dw, gm, um, dm,
    ig, gwg, uwg, dwg,
    zin, allt, allo, wcat, wdown, keep,
    zl_gu_out, zl_gu_in, zl_b_out, zl_b_in, sum_gu, sum_b,
    x_gu_out, x_gu_in, x_b_out, x_b_in, gu, hid,
    core_out, core_in, own, y_out, y_in, z_out, z_in,
    az_s, az_r, ay_s, ay_r, ac_s, ac_r,
    bz_s, bz_r, bx_s, bx_r,
    cx_s, cx_r, cz_s, cz_r,
    dc_s, dc_r, dy_s, dy_r, dz_s, dz_r,
):
    nx, nl, ny, nz, nc = dims
    row, col = lax.axis_index("row"), lax.axis_index("col")
    x, zl = row // nl, row % nl
    core = col % nc
    z = (col // nc) % nz
    y = col // (nc * nz)
    height, width = dw.shape
    rows = tok.shape[0]
    half = ny * TILE

    def x_peer(by):
        return (lax.rem(x + by, nx) * nl + zl, col)

    def y_peer(by):
        return (row, (lax.rem(y + by, ny) * nz + z) * nc + core)

    def z_peer(by):
        return (row, (y * nz + lax.rem(z + by, nz)) * nc + core)

    zl_peer = (x * nl + (1 - zl), col)
    core_peer = (row, (y * nz + z) * nc + (1 - core))

    peers = [x_peer(by) for by in range(1, nx)] + [y_peer(by) for by in range(1, ny)]
    peers += [z_peer(by) for by in range(1, nz)] + [zl_peer, core_peer]
    barrier = pltpu.get_barrier_semaphore()
    for peer in peers:
        pl.semaphore_signal(barrier, inc=1, device_id=peer, device_id_type=MESH)

    started = []

    def send(src, dst, s, r, peer):
        copy = pltpu.make_async_remote_copy(
            src_ref=src, dst_ref=dst, send_sem=s, recv_sem=r,
            device_id=peer, device_id_type=MESH,
        )
        copy.start()
        started.append(copy)
        return copy

    def block(at):
        return pl.ds(pl.multiple_of(at * TILE, TILE), TILE)

    def part(at):
        return pl.ds(pl.multiple_of(at * half, half), half)

    def order(n):
        return sorted(range(1, n), key=lambda by: min(by, n - by))

    gate_keep = expanded(gm[...], True, width, height)
    keep[pl.ds(0, height), :] = gate_keep.astype(BF16)
    wcat[pl.ds(0, height), :] = (gw[...].astype(F32) * gate_keep).astype(BF16)

    pl.semaphore_wait(barrier, len(peers))

    az = [
        [send(ref, zin.at[k, z], az_s.at[k, by], az_r.at[k, by], z_peer(by)) for by in range(1, nz)]
        for k, ref in enumerate((tok, og))
    ]

    up_keep = expanded(um[...], True, width, height)
    keep[pl.ds(height, height), :] = up_keep.astype(BF16)
    wcat[pl.ds(height, height), :] = (uw[...].astype(F32) * up_keep).astype(BF16)

    ay, ac = [], []
    for k, (ref, full) in enumerate(((tok, allt), (og, allo))):
        zin[k, z] = ref[...]
        for copy in az[k]:
            copy.wait_recv()
        gathered = jnp.concatenate([zin[k, i].astype(F32) for i in range(nz)], axis=0)
        here = block(core * ny + y)
        full[here, :] = gathered.astype(BF16)
        ay.append(
            {
                by: send(full.at[here, :], full.at[here, :], ay_s.at[k, by], ay_r.at[k, by], y_peer(by))
                for by in order(ny)
            }
        )
        ac.append([send(full.at[here, :], full.at[here, :], ac_s.at[k, 0], ac_r.at[k, 0], core_peer)])

    down_keep = expanded(dm[...], False, width, height)
    keep[pl.ds(2 * height, height), :] = down_keep.astype(BF16)
    wdown[...] = (dw[...].astype(F32) * down_keep).astype(BF16)

    def finish_gather(k, full):
        for by in order(ny):
            ay[k][by].wait_recv()
            there = block(core * ny + lax.rem(y + ny - by, ny))
            ac[k].append(
                send(full.at[there, :], full.at[there, :], ac_s.at[k, by], ac_r.at[k, by], core_peer)
            )
        for copy in ac[k]:
            copy.wait_recv()

    finish_gather(0, allt)
    zl_gu_out[...] = dot(allt[part(1 - zl), :], wcat[...], (1, 1)).astype(BF16)
    bz_gu = send(zl_gu_out, zl_gu_in, bz_s.at[0], bz_r.at[0], zl_peer)
    sum_gu[...] = dot(allt[part(zl), :], wcat[...], (1, 1))
    finish_gather(1, allo)
    zl_b_out[...] = dot(allo[part(1 - zl), :], wdown[...], (1, 1)).astype(BF16)
    bz_b = send(zl_b_out, zl_b_in, bz_s.at[1], bz_r.at[1], zl_peer)
    sum_b[...] = dot(allo[part(zl), :], wdown[...], (1, 1))

    bx = []
    for k, (first, arrived, total, out, into) in enumerate(
        ((bz_gu, zl_gu_in, sum_gu, x_gu_out, x_gu_in), (bz_b, zl_b_in, sum_b, x_b_out, x_b_in))
    ):
        first.wait_recv()
        paired = total[...] + arrived[...].astype(F32)
        total[...] = paired
        out[...] = paired.astype(BF16)
        bx.append(
            [
                send(out.at[block(lax.rem(x + by, nx)), :], into.at[by], bx_s.at[k, by], bx_r.at[k, by], x_peer(by))
                for by in order(nx)
            ]
        )

    sums = []
    for k, (total, into) in enumerate(((sum_gu, x_gu_in), (sum_b, x_b_in))):
        value = total[block(x), :]
        for copy, by in zip(bx[k], order(nx)):
            copy.wait_recv()
            value = value + into[by].astype(F32)
        sums.append(value)

    gate, up, back = sums[0][:, :height], sums[0][:, height:], sums[1]
    logistic = 1.0 / (1.0 + jnp.exp(-gate))
    swish = gate * logistic
    up_grad = back * swish
    gate_grad = back * up * logistic * (1.0 + gate * (1.0 - logistic))
    mine = block(zl * nx + x)
    gu[mine, :] = jnp.concatenate([gate_grad, up_grad], axis=1).astype(BF16)
    hid[mine, :] = (swish * up).astype(BF16)

    cx, cz = [], []
    for k, full in enumerate((gu, hid)):
        cx.append(
            {
                by: send(full.at[mine, :], full.at[mine, :], cx_s.at[k, by], cx_r.at[k, by], x_peer(by))
                for by in order(nx)
            }
        )
        cz.append([send(full.at[mine, :], full.at[mine, :], cz_s.at[k, 0], cz_r.at[k, 0], zl_peer)])
    for k, full in enumerate((gu, hid)):
        for by in order(nx):
            cx[k][by].wait_recv()
            there = block(zl * nx + lax.rem(x + nx - by, nx))
            cz[k].append(
                send(full.at[there, :], full.at[there, :], cz_s.at[k, by], cz_r.at[k, by], zl_peer)
            )
        if k == 0:
            for copy in cz[k]:
                copy.wait_recv()
            core_out[...] = dot(gu[part(1 - core), :], wcat[...], (1, 0))
            dc = send(core_out, core_in, dc_s, dc_r, core_peer)
            own[...] = dot(gu[part(core), :], wcat[...], (1, 0))

    dc.wait_recv()
    total = own[...] + core_in[...]
    own[...] = total
    y_out[...] = total.astype(BF16)
    dy = [
        send(y_out.at[block(lax.rem(y + by, ny)), :], y_in.at[by], dy_s.at[by], dy_r.at[by], y_peer(by))
        for by in order(ny)
    ]

    gwg[...] = (dot(gu[:, :height], allt[...], (0, 0)) * keep[pl.ds(0, height), :].astype(F32)).astype(BF16)
    uwg[...] = (dot(gu[:, height:], allt[...], (0, 0)) * keep[pl.ds(height, height), :].astype(F32)).astype(BF16)

    value = own[block(y), :]
    for copy, by in zip(dy, order(ny)):
        copy.wait_recv()
        value = value + y_in[by].astype(F32)
    for i in range(nz):
        z_out[i] = value[i * rows : (i + 1) * rows, :]
    dz = [
        send(z_out.at[lax.rem(z + by, nz)], z_in.at[by], dz_s.at[by], dz_r.at[by], z_peer(by))
        for by in range(1, nz)
    ]

    for copy in cz[1]:
        copy.wait_recv()
    dwg[...] = (dot(hid[...], allo[...], (0, 0)) * keep[pl.ds(2 * height, height), :].astype(F32)).astype(BF16)

    final = z_out[z]
    for copy, by in zip(dz, range(1, nz)):
        copy.wait_recv()
        final = final + z_in[by]
    ig[...] = final.astype(BF16)

    for copy in started:
        copy.wait_send()


def local(dims, tokens, out_grad, gate_weight, up_weight, down_weight, gate_mask, up_mask, down_mask):
    nx, nl, ny, nz, nc = dims
    rows, width = tokens.shape
    height = down_weight.shape[0]
    half = ny * TILE
    dma = pltpu.SemaphoreType.DMA
    vmem = pl.BlockSpec(memory_space=pltpu.VMEM)
    weight = jax.ShapeDtypeStruct((height, width), BF16)
    scratch = [
        pltpu.VMEM((2, nz, rows, width), BF16),
        pltpu.VMEM((2 * half, width), BF16),
        pltpu.VMEM((2 * half, width), BF16),
        pltpu.VMEM((2 * height, width), BF16),
        pltpu.VMEM((height, width), BF16),
        pltpu.VMEM((3 * height, width), BF16),
        pltpu.VMEM((half, 2 * height), BF16),
        pltpu.VMEM((half, 2 * height), BF16),
        pltpu.VMEM((half, height), BF16),
        pltpu.VMEM((half, height), BF16),
        pltpu.VMEM((half, 2 * height), F32),
        pltpu.VMEM((half, height), F32),
        pltpu.VMEM((half, 2 * height), BF16),
        pltpu.VMEM((nx, TILE, 2 * height), BF16),
        pltpu.VMEM((half, height), BF16),
        pltpu.VMEM((nx, TILE, height), BF16),
        pltpu.VMEM((2 * half, 2 * height), BF16),
        pltpu.VMEM((2 * half, height), BF16),
        pltpu.VMEM((half, width), F32),
        pltpu.VMEM((half, width), F32),
        pltpu.VMEM((half, width), F32),
        pltpu.VMEM((half, width), BF16),
        pltpu.VMEM((ny, TILE, width), BF16),
        pltpu.VMEM((nz, rows, width), F32),
        pltpu.VMEM((nz, rows, width), F32),
        dma((2, nz)), dma((2, nz)), dma((2, ny)), dma((2, ny)), dma((2, ny)), dma((2, ny)),
        dma((2,)), dma((2,)), dma((2, nx)), dma((2, nx)),
        dma((2, nx)), dma((2, nx)), dma((2, nx)), dma((2, nx)),
        dma, dma, dma((ny,)), dma((ny,)), dma((nz,)), dma((nz,)),
    ]
    input_grad, gate_wg, up_wg, down_wg = pl.pallas_call(
        functools.partial(kernel, dims),
        out_shape=(jax.ShapeDtypeStruct((rows, width), BF16), weight, weight, weight),
        in_specs=[vmem] * 8,
        out_specs=(vmem,) * 4,
        scratch_shapes=scratch,
        compiler_params=pltpu.CompilerParams(
            collective_id=0, has_side_effects=True, vmem_limit_bytes=40 * 1024 * 1024
        ),
        name="block",
    )(
        tokens, out_grad, gate_weight.T, up_weight.T, down_weight,
        gate_mask, up_mask, down_mask.T,
    )
    return input_grad, gate_wg.T, up_wg.T, down_wg


def solution(mesh, dims=(8, 2, 8, 4, 2)):
    in_specs = (
        P("col", "row"),
        P("col", "row"),
        P("row", "col"),
        P("row", "col"),
        P("col", "row"),
        P("row", "col"),
        P("row", "col"),
        P("col", "row"),
    )
    out_specs = (P("col", "row"), P("row", "col"), P("row", "col"), P("col", "row"))
    return jax.shard_map(
        functools.partial(local, dims), mesh=mesh, in_specs=in_specs, out_specs=out_specs, check_vma=False
    )
```

time: 215 us -> 89.8 us (0.42)
  blocking collectives: 163 us -> 0 us
  Pallas kernels: 0 us -> 78.5 us
  waiting for transfers between devices: 17.1 us -> 0 us
  other arithmetic: 9.24 us -> 0 us
  starting transfers between devices: 6.66 us -> 0 us
  matrix products: 6 us -> 0 us
    all_gather x1 -> x0, blocking collectives: 97.6 us -> none  [sent_together(): lax.all_gather(both, axis, axis=dim, tiled=True)]
    pallas_call x0 -> x1, Pallas kernels: none -> 78.5 us  [local(): pl.pallas_call(functools.partial(kernel, dims), out_shape=(jax.ShapeDtype...]
    all_to_all x2 -> x0, blocking collectives: 65 us -> none  [the longest x1 42 us: summed_on_arrival(): lax.all_to_all(pieces, axis, split_axis=0, concat_axis=0, tiled=True)]
    all_to_all x1 -> x0, waiting for transfers between devices: 17.1 us -> none  [summed_on_arrival(): lax.all_to_all(pieces, axis, split_axis=0, concat_axis=0, tiled=True)]
    unnamed x21 -> x20, local copies, waits for them, and re-layouts: 1.47 us -> 10.1 us
    all_to_all x1 -> x0, starting transfers between devices: 6.66 us -> none  [summed_on_arrival(): lax.all_to_all(pieces, axis, split_axis=0, concat_axis=0, tiled=True)]
    dot_general x8 -> x0, matrix products: 6 us -> none  [the longest x3 3.86 us: contract_first(): lax.dot_general(left, right, (((0,), (0,)), ((), ())), preferred_element_...]
    reshape x14 -> x0, local copies, waits for them, and re-layouts: 4 us -> none  [the longest x5 1.79 us: expand_mask(): jnp.stack(row_list, axis=1).reshape(4 * group_rows, 4 * group_cols)]
  transfers between devices with their start and end apart: 1 -> 0, of which waited for: 1 -> 0; matrix products, arithmetic and copies ran while one was open for 2% -> 0% of each run, Pallas kernels for 0% -> 0%
where the time goes in v1:
time: 89.8 us; the launch traced here: 89.3 us
  Pallas kernels  78.5 us (87%)
  local copies, waits for them, and re-layouts  10.1 us (11%)
    pallas_call x1, Pallas kernels, local(): pl.pallas_call(functools.partial(kernel, dims), out_shape=(jax.ShapeDtype...  78.5 us
    unnamed x20, local copies, waits for them, and re-layouts  10.1 us

profile of v1, /device:TPU:1, one launch (start us, length us, event | category | flops | bytes accessed | tf_op | source)
XLA Modules:
  0.0 89.3 jit_solution(2117144164904711689)
XLA Ops:
  0.6 0.0 copy-start.6
  0.6 0.7 copy-done.6
  1.3 0.0 copy-start
  1.3 1.0 %copy-done = bf16[640,416]{0,1:T(8,128)(2,1)S(1)} copy-done((bf16[640,416]{0,1:T(8,128)(2,1)S(1)}, bf16[640,416]{0,1:T(8,128)(2,1)}, u32[]{:S(2)}) %copy-start) | copy-done | bytes 532504
  2.4 0.0 copy-start.1
  2.4 1.0 %copy-done.1 = bf16[640,416]{0,1:T(8,128)(2,1)S(1)} copy-done((bf16[640,416]{0,1:T(8,128)(2,1)S(1)}, bf16[640,416]{0,1:T(8,128)(2,1)}, u32[]{:S(2)}) %copy-start.1) | copy-done | bytes 532504
  3.4 0.0 copy-start.2
  3.4 1.0 %copy-done.2 = bf16[416,640]{1,0:T(8,128)(2,1)S(1)} copy-done((bf16[416,640]{1,0:T(8,128)(2,1)S(1)}, bf16[416,640]{1,0:T(8,128)(2,1)}, u32[]{:S(2)}) %copy-start.2) | copy-done | bytes 532504
  4.5 0.0 copy-start.3
  4.5 0.9 copy-done.3
  5.3 0.0 copy-start.4
  5.3 0.9 copy-done.4
  6.2 0.0 copy-start.5
  6.2 0.9 copy-done.5
  7.1 0.0 copy-start.7
  7.1 0.7 copy-done.7
  7.8 78.5 %block.1 = (bf16[4,640]{1,0:T(4,128)(2,1)S(1)}, bf16[416,640]{1,0:T(8,128)(2,1)S(1)}, bf16[416,640]{1,0:T(8,128)(2,1)S(1)}, bf16[416,640]{1,0:T(8,128)(2,1)S(1)}) custom-call(bf16[4,640]{1,0:T(4,128)(2,1)S(1)} %copy-done.6, bf16[4,640]{1,0:T(4,128)(2,1)S(1)} %copy-done.7, bf16[416,640]{1,0:T(8,128)(2,1)S(1)} %bitcast.7, bf16[416,640]{1,0:T(8,128)(2,1)S(1)} %bitcast.8, ...), custom_call_target="tpu_custom_call" | custom-call | tf_op jit(solution)/shard_map/block/pallas_call | solution.py:316
  86.3 0.6 copy.16
  86.9 0.8 copy.17
  87.7 0.8 copy.18
  88.5 0.8 copy.19
Async XLA Ops:
  0.6 0.7 copy-start.6
  1.3 1.0 %copy-start = (bf16[640,416]{0,1:T(8,128)(2,1)S(1)}, bf16[640,416]{0,1:T(8,128)(2,1)}, u32[]{:S(2)}) copy-start(bf16[640,416]{0,1:T(8,128)(2,1)} %param.10) | copy-start | bytes 1597444
  2.4 1.0 %copy-start.1 = (bf16[640,416]{0,1:T(8,128)(2,1)S(1)}, bf16[640,416]{0,1:T(8,128)(2,1)}, u32[]{:S(2)}) copy-start(bf16[640,416]{0,1:T(8,128)(2,1)} %param.11) | copy-start | bytes 1597444
  3.4 1.0 %copy-start.2 = (bf16[416,640]{1,0:T(8,128)(2,1)S(1)}, bf16[416,640]{1,0:T(8,128)(2,1)}, u32[]{:S(2)}) copy-start(bf16[416,640]{1,0:T(8,128)(2,1)} %dw.1) | copy-start | bytes 1597444
  4.5 0.9 copy-start.3
  5.3 0.9 copy-start.4
  6.2 0.9 copy-start.5
  7.1 0.7 copy-start.7

commit v2 on v1

v2 whole, which is shorter than its diff:
```python
import functools

import jax
import jax.numpy as jnp
from jax import lax
from jax.experimental import pallas as pl
from jax.experimental.pallas import tpu as pltpu
from jax.sharding import PartitionSpec as P

F32 = jnp.float32
BF16 = jnp.bfloat16
MESH = pl.DeviceIdType.MESH
TILE = 16


def dot(left, right, at):
    return lax.dot_general(
        left, right, (((at[0],), (at[1],)), ((), ())), preferred_element_type=F32
    )


def orderings(code):
    def step(value, bound):
        return (value >= bound).astype(jnp.int32)

    p0 = step(code, 6) + step(code, 12) + step(code, 18)
    rest = code - 6 * p0
    rank1 = step(rest, 2) + step(rest, 4)
    rank2 = rest - 2 * rank1
    p1 = rank1 + (rank1 >= p0).astype(jnp.int32)
    low, high = jnp.minimum(p0, p1), jnp.maximum(p0, p1)
    rest_low = jnp.where(low > 0, 0, jnp.where(high > 1, 1, 2))
    rest_high = 6 - low - high - rest_low
    p2 = jnp.where(rank2 == 0, rest_low, rest_high)
    return p0, p1, p2, 6 - p0 - p1 - p2


def nibbles(code, bits_are_columns):
    p = orderings(code)
    one = jnp.ones_like(code)
    kept = []
    for at in range(4):
        if bits_are_columns:
            kept.append((one << p[at]) | (one << p[(at + 1) % 4]))
        else:
            bits = jnp.zeros_like(code)
            for i in range(4):
                hit = (p[i] == at) | (p[(i + 1) % 4] == at)
                bits = bits | jnp.where(hit, 1 << i, 0)
            kept.append(bits)
    return [k.astype(F32).astype(BF16) for k in kept]


def expanded(code, bits_are_columns, width, height):
    quarter = width // 4
    parts = nibbles(code, bits_are_columns)
    wide = jnp.zeros((code.shape[1], width), F32)
    d = lax.broadcasted_iota(jnp.int32, (quarter, width), 1)
    a = lax.broadcasted_iota(jnp.int32, (quarter, width), 0)
    for i in range(4):
        spread = (d == 4 * a + i).astype(F32).astype(BF16)
        wide = wide + dot(parts[i], spread, (0, 0))
    f = lax.broadcasted_iota(jnp.int32, (height, height // 4), 0)
    b = lax.broadcasted_iota(jnp.int32, (height, height // 4), 1)
    tall = dot(((f >> 2) == b).astype(F32).astype(BF16), wide.astype(BF16), (1, 0))
    local = lax.broadcasted_iota(jnp.int32, (height, width), 0) & 3
    return ((tall.astype(jnp.int32) >> local) & 1).astype(F32)


def routes(n):
    if n < 4:
        return list(range(1, n)), {}
    if n == 4:
        return [1, 3], {1: [2]}
    return [2, 6, 1, 7], {2: [3, 4], 6: [5]}


def kernel(
    dims,
    tok, og, gw, uw, dw, gm, um, dm,
    ig, gwg, uwg, dwg,
    zin, allt, allo, wcat, wdown, keep, codes,
    zl_gu_out, zl_gu_in, zl_b_out, zl_b_in, sum_gu, sum_b,
    x_gu_out, x_gu_in, x_b_out, x_b_in, gu, hid,
    core_out, core_in, own, y_out, y_in, z_out, z_in,
    load, sent, az_r, ay_r, ac_r, bz_r, bx_r, cx_r, cz_r, d_r,
):
    nx, nl, ny, nz, nc = dims
    row, col = lax.axis_index("row"), lax.axis_index("col")
    x, zl = row // nl, row % nl
    core = col % nc
    z = (col // nc) % nz
    y = col // (nc * nz)
    hand = 1 - 2 * core
    height, width = dw.shape
    rows = tok.shape[0]
    half = ny * TILE

    def x_peer(by):
        return (lax.rem(x + nx + by, nx) * nl + zl, col)

    def y_peer(by):
        return (row, (lax.rem(y + ny + by, ny) * nz + z) * nc + core)

    def z_peer(by):
        return (row, (y * nz + lax.rem(z + by, nz)) * nc + core)

    zl_peer = (x * nl + (1 - zl), col)
    core_peer = (row, (y * nz + z) * nc + (1 - core))

    peers = [y_peer(by) for by in range(1, ny)] + [x_peer(by) for by in range(1, nx)]
    peers += [z_peer(by) for by in range(1, nz)] + [zl_peer, core_peer]
    barrier = pltpu.get_barrier_semaphore()
    for peer in peers:
        pl.semaphore_signal(barrier, inc=1, device_id=peer, device_id_type=MESH)

    loads = [
        pltpu.make_async_copy(src, dst, load.at[i])
        for i, (src, dst) in enumerate(
            (
                (gm, codes.at[0]),
                (gw, wcat.at[pl.ds(0, height), :]),
                (um, codes.at[1]),
                (uw, wcat.at[pl.ds(height, height), :]),
                (dm, codes.at[2]),
                (dw, wdown),
                (tok, zin.at[0, z]),
                (og, zin.at[1, z]),
            )
        )
    ]
    for copy in loads:
        copy.start()

    def send(src, dst, s, r, peer):
        pltpu.make_async_remote_copy(
            src_ref=src, dst_ref=dst, send_sem=s, recv_sem=r,
            device_id=peer, device_id_type=MESH,
        ).start()

    def settle(ref, semaphore):
        pltpu.make_async_copy(ref, ref, semaphore).wait()

    def block(at):
        return pl.ds(pl.multiple_of(at * TILE, TILE), TILE)

    def part(at):
        return pl.ds(pl.multiple_of(at * half, half), half)

    def far_first(n):
        return sorted(range(1, n), key=lambda by: -min(by, n - by))

    def spread(full, base, me, n, peer, s, r, f_r, f_peer):
        direct, relays = routes(n)

        def rows_of(at):
            return full.at[block(base + at), :]

        def first():
            mine = rows_of(me)
            for by in direct:
                send(mine, mine, s, r.at[by], peer(hand * by))
            send(mine, mine, s, f_r, f_peer)

        def take(offsets):
            for by in offsets:
                there = rows_of(lax.rem(me + n * n - hand * by, n))
                settle(there, r.at[by])
                for onward in relays.get(by, []):
                    send(there, there, s, r.at[onward], peer(hand * (onward - by)))
                send(there, there, s, f_r, f_peer)

        def rest():
            settle(full.at[pl.ds(0, half), :], f_r)

        def drained():
            settle(full.at[pl.ds(0, (2 * n - 1) * TILE), :], s)

        via = [by for by in direct if by in relays]
        near = [by for by in direct if by not in relays]
        far = [by for by in range(1, n) if by not in direct]
        return first, take, rest, drained, (via, near, sorted(far, key=lambda by: min(by, n - by)))

    def prepared(i, dst, at):
        kept = expanded(codes[i], i < 2, width, height)
        keep[pl.ds(i * height, height), :] = kept.astype(BF16)
        dst[at, :] = (dst[at, :].astype(F32) * kept).astype(BF16)

    pl.semaphore_wait(barrier, len(peers))

    for k, ref in enumerate((tok, og)):
        for by in range(1, nz):
            send(ref, zin.at[k, z], sent.at[k], az_r.at[k], z_peer(by))

    loads[0].wait()
    loads[1].wait()
    prepared(0, wcat, pl.ds(0, height))
    loads[2].wait()
    loads[3].wait()
    prepared(1, wcat, pl.ds(height, height))

    t_first, t_take, t_rest, t_drained, t_at = spread(
        allt, core * ny, y, ny, y_peer, sent.at[2], ay_r.at[0], ac_r.at[0], core_peer
    )
    o_first, o_take, o_rest, o_drained, o_at = spread(
        allo, core * ny, y, ny, y_peer, sent.at[3], ay_r.at[1], ac_r.at[1], core_peer
    )
    for k, (full, first) in enumerate(((allt, t_first), (allo, o_first))):
        loads[6 + k].wait()
        if nz > 1:
            settle(zin.at[k, pl.ds(0, nz - 1)], az_r.at[k])
        gathered = jnp.concatenate([zin[k, i].astype(F32) for i in range(nz)], axis=0)
        full[block(core * ny + y), :] = gathered.astype(BF16)
        first()

    loads[4].wait()
    loads[5].wait()
    prepared(2, wdown, pl.ds(0, height))

    t_take(t_at[0])
    t_take(t_at[1])
    o_take(o_at[0])
    t_take(t_at[2])
    t_rest()

    def owed(total, out, into, k, full, weight):
        out[...] = dot(full[part(1 - zl), :], weight[...], (1, 1)).astype(BF16)
        for by in far_first(nx) + [0]:
            there = block(lax.rem(x + by, nx))
            send(out.at[there, :], into.at[there, :], sent.at[4 + k], bz_r.at[k, by], zl_peer)
        total[...] = dot(full[part(zl), :], weight[...], (1, 1))

    owed(sum_gu, zl_gu_out, zl_gu_in, 0, allt, wcat)
    o_take(o_at[1])
    o_take(o_at[2])
    o_rest()
    owed(sum_b, zl_b_out, zl_b_in, 1, allo, wdown)

    parts = ((sum_gu, zl_gu_in, x_gu_out, x_gu_in), (sum_b, zl_b_in, x_b_out, x_b_in))
    for k, (total, arrived, out, into) in enumerate(parts):
        for by in far_first(nx):
            there = block(lax.rem(x + by, nx))
            settle(arrived.at[there, :], bz_r.at[k, by])
            out[there, :] = (total[there, :] + arrived[there, :].astype(F32)).astype(BF16)
            send(out.at[there, :], into.at[by], sent.at[6 + k], bx_r.at[k], x_peer(by))

    sums = []
    for k, (total, arrived, out, into) in enumerate(parts):
        here = block(x)
        settle(arrived.at[here, :], bz_r.at[k, 0])
        value = total[here, :] + arrived[here, :].astype(F32)
        settle(into.at[pl.ds(1, nx - 1)], bx_r.at[k])
        for by in range(1, nx):
            value = value + into[by].astype(F32)
        sums.append(value)

    gate, up, back = sums[0][:, :height], sums[0][:, height:], sums[1]
    logistic = 1.0 / (1.0 + jnp.exp(-gate))
    swish = gate * logistic
    up_grad = back * swish
    gate_grad = back * up * logistic * (1.0 + gate * (1.0 - logistic))
    mine = block(zl * nx + x)
    gu[mine, :] = jnp.concatenate([gate_grad, up_grad], axis=1).astype(BF16)
    g_first, g_take, g_rest, g_drained, g_at = spread(
        gu, zl * nx, x, nx, x_peer, sent.at[8], cx_r.at[0], cz_r.at[0], zl_peer
    )
    h_first, h_take, h_rest, h_drained, h_at = spread(
        hid, zl * nx, x, nx, x_peer, sent.at[9], cx_r.at[1], cz_r.at[1], zl_peer
    )
    g_first()
    hid[mine, :] = (swish * up).astype(BF16)
    g_take(g_at[0])
    h_first()
    g_take(g_at[1])
    g_take(g_at[2])
    h_take(h_at[0])
    g_rest()

    core_out[...] = dot(gu[part(1 - core), :], wcat[...], (1, 0))
    send(core_out, core_in, sent.at[10], d_r.at[0], core_peer)
    own[...] = dot(gu[part(core), :], wcat[...], (1, 0))
    h_take(h_at[1])
    settle(core_in, d_r.at[0])
    total = own[...] + core_in[...]
    own[...] = total
    y_out[...] = total.astype(BF16)
    for by in far_first(ny):
        send(y_out.at[block(lax.rem(y + by, ny)), :], y_in.at[by], sent.at[11], d_r.at[1], y_peer(by))
    h_take(h_at[2])

    gwg[...] = (dot(gu[:, :height], allt[...], (0, 0)) * keep[pl.ds(0, height), :].astype(F32)).astype(BF16)
    uwg[...] = (dot(gu[:, height:], allt[...], (0, 0)) * keep[pl.ds(height, height), :].astype(F32)).astype(BF16)
    h_rest()

    value = own[block(y), :]
    settle(y_in.at[pl.ds(1, ny - 1)], d_r.at[1])
    for by in range(1, ny):
        value = value + y_in[by].astype(F32)
    for i in range(nz):
        z_out[i] = value[i * rows : (i + 1) * rows, :]
    for by in range(1, nz):
        send(z_out.at[lax.rem(z + by, nz)], z_in.at[by], sent.at[12], d_r.at[2], z_peer(by))

    dwg[...] = (dot(hid[...], allo[...], (0, 0)) * keep[pl.ds(2 * height, height), :].astype(F32)).astype(BF16)
    for k in range(2):
        if nz > 1:
            settle(zin.at[k, pl.ds(0, nz - 1)], sent.at[k])
    for drained in (t_drained, o_drained, g_drained, h_drained):
        drained()
    settle(zl_gu_out, sent.at[4])
    settle(zl_b_out, sent.at[5])
    settle(x_gu_out.at[pl.ds(0, (nx - 1) * TILE), :], sent.at[6])
    settle(x_b_out.at[pl.ds(0, (nx - 1) * TILE), :], sent.at[7])
    settle(core_out, sent.at[10])
    settle(y_out.at[pl.ds(0, (ny - 1) * TILE), :], sent.at[11])

    final = z_out[z]
    if nz > 1:
        settle(z_in.at[pl.ds(1, nz - 1)], d_r.at[2])
    for by in range(1, nz):
        final = final + z_in[by]
    ig[...] = final.astype(BF16)
    if nz > 1:
        settle(z_out.at[pl.ds(0, nz - 1)], sent.at[12])


def written(*refs):
    done = refs[-1]
    copies = [
        pltpu.make_async_copy(refs[i], refs[i + 4], done.at[i]) for i in range(4)
    ]
    for copy in copies:
        copy.start()
    for copy in copies:
        copy.wait()


def local(dims, tokens, out_grad, gate_weight, up_weight, down_weight, gate_mask, up_mask, down_mask):
    nx, nl, ny, nz, nc = dims
    rows, width = tokens.shape
    height = down_weight.shape[0]
    half = ny * TILE
    dma = pltpu.SemaphoreType.DMA
    vmem = pl.BlockSpec(memory_space=pltpu.VMEM)
    weight = jax.ShapeDtypeStruct((height, width), BF16)
    scratch = [
        pltpu.VMEM((2, nz, rows, width), BF16),
        pltpu.VMEM((2 * half, width), BF16),
        pltpu.VMEM((2 * half, width), BF16),
        pltpu.VMEM((2 * height, width), BF16),
        pltpu.VMEM((height, width), BF16),
        pltpu.VMEM((3 * height, width), BF16),
        pltpu.VMEM((3, width // 4, height // 4), jnp.int32),
        pltpu.VMEM((half, 2 * height), BF16),
        pltpu.VMEM((half, 2 * height), BF16),
        pltpu.VMEM((half, height), BF16),
        pltpu.VMEM((half, height), BF16),
        pltpu.VMEM((half, 2 * height), F32),
        pltpu.VMEM((half, height), F32),
        pltpu.VMEM((half, 2 * height), BF16),
        pltpu.VMEM((nx, TILE, 2 * height), BF16),
        pltpu.VMEM((half, height), BF16),
        pltpu.VMEM((nx, TILE, height), BF16),
        pltpu.VMEM((2 * half, 2 * height), BF16),
        pltpu.VMEM((2 * half, height), BF16),
        pltpu.VMEM((half, width), F32),
        pltpu.VMEM((half, width), F32),
        pltpu.VMEM((half, width), F32),
        pltpu.VMEM((half, width), BF16),
        pltpu.VMEM((ny, TILE, width), BF16),
        pltpu.VMEM((nz, rows, width), F32),
        pltpu.VMEM((nz, rows, width), F32),
        dma((8,)), dma((13,)), dma((2,)), dma((2, ny)), dma((2,)),
        dma((2, nx)), dma((2,)), dma((2, nx)), dma((2,)), dma((3,)),
    ]
    held = (jax.ShapeDtypeStruct((rows, width), BF16), weight, weight, weight)
    results = pl.pallas_call(
        functools.partial(kernel, dims),
        out_shape=held,
        in_specs=[pl.BlockSpec(memory_space=pltpu.HBM)] * 8,
        out_specs=(vmem,) * 4,
        scratch_shapes=scratch,
        compiler_params=pltpu.CompilerParams(
            collective_id=0, has_side_effects=True, vmem_limit_bytes=40 * 1024 * 1024
        ),
        name="block",
    )(
        *(
            pltpu.with_memory_space_constraint(a, pltpu.HBM)
            for a in (
                tokens, out_grad, gate_weight.T, up_weight.T, down_weight,
                gate_mask, up_mask, down_mask.T,
            )
        )
    )
    input_grad, gate_wg, up_wg, down_wg = pl.pallas_call(
        written,
        out_shape=held,
        in_specs=[pl.BlockSpec(memory_space=pl.ANY)] * 4,
        out_specs=(pl.BlockSpec(memory_space=pl.ANY),) * 4,
        scratch_shapes=[dma((4,))],
        compiler_params=pltpu.CompilerParams(vmem_limit_bytes=2 * 1024 * 1024),
        name="write",
    )(*results)
    return input_grad, gate_wg.T, up_wg.T, down_wg


def solution(mesh, dims=(8, 2, 8, 4, 2)):
    in_specs = (
        P("col", "row"),
        P("col", "row"),
        P("row", "col"),
        P("row", "col"),
        P("col", "row"),
        P("row", "col"),
        P("row", "col"),
        P("col", "row"),
    )
    out_specs = (P("col", "row"), P("row", "col"), P("row", "col"), P("col", "row"))
    return jax.shard_map(
        functools.partial(local, dims), mesh=mesh, in_specs=in_specs, out_specs=out_specs, check_vma=False
    )
```

time: 89.8 us -> 73.5 us (0.82)
  local copies, waits for them, and re-layouts: 10.1 us -> 0 us
  Pallas kernels: 78.5 us -> 72.7 us
    unnamed x20 -> x0, local copies, waits for them, and re-layouts: 10.1 us -> none
    pallas_call x1 -> x2, Pallas kernels: 78.5 us -> 72.7 us  [the longest x1 71.5 us: local(): pl.pallas_call(functools.partial(kernel, dims), out_shape=held, in_specs=...]
where the time goes in v2:
time: 73.5 us; the launch traced here: 73.4 us
  Pallas kernels  72.7 us (99%)
    pallas_call x1, Pallas kernels, local(): pl.pallas_call(functools.partial(kernel, dims), out_shape=held, in_specs=...  71.5 us

profile of v2, /device:TPU:1, one launch (start us, length us, event | category | flops | bytes accessed | tf_op | source)
XLA Modules:
  0.0 73.4 jit_solution(6090870650881417919)
XLA Ops:
  0.6 71.5 %block.1 = (bf16[4,640]{1,0:T(4,128)(2,1)S(1)}, bf16[416,640]{1,0:T(8,128)(2,1)S(1)}, bf16[416,640]{1,0:T(8,128)(2,1)S(1)}, bf16[416,640]{1,0:T(8,128)(2,1)S(1)}) custom-call(bf16[4,640]{1,0:T(4,128)(2,1)} %tok.1, bf16[4,640]{1,0:T(4,128)(2,1)} %og.1, bf16[416,640]{1,0:T(8,128)(2,1)} %bitcast.5, bf16[416,640]{1,0:T(8,128)(2,1)} %bitcast.6, ...), custom_call_target="tpu_custom_call" | custom-call | tf_op jit(solution)/shard_map/block/pallas_call | solution.py:377
  72.2 1.2 %write.1 = (bf16[4,640]{1,0:T(4,128)(2,1)}, bf16[416,640]{1,0:T(8,128)(2,1)}, bf16[416,640]{1,0:T(8,128)(2,1)}, bf16[416,640]{1,0:T(8,128)(2,1)}) custom-call(bf16[4,640]{1,0:T(4,128)(2,1)S(1)} %get-tuple-element.12.refs_0_, bf16[416,640]{1,0:T(8,128)(2,1)S(1)} %get-tuple-element.13.refs_1_, bf16[416,640]{1,0:T(8,128)(2,1)S(1)} %get-tuple-element.14.refs_2_, ...), custom_call_target="tpu_custom_call" | custom-call | tf_op jit(solution)/shard_map/write/pallas_call | solution.py:396

commit v3 on v2

--- a/solution.py
+++ b/solution.py
@@ -93,6 +93,7 @@
     y = col // (nc * nz)
     hand = 1 - 2 * core
     height, width = dw.shape
+    width_of = (sum_gu.shape[1], sum_b.shape[1])
     rows = tok.shape[0]
     half = ny * TILE
 
@@ -150,7 +151,7 @@
     def far_first(n):
         return sorted(range(1, n), key=lambda by: -min(by, n - by))
 
-    def spread(full, base, me, n, peer, s, r, f_r, f_peer):
+    def spread(full, base, me, n, peer, s, r, f_r, f_peer, straight=False):
         direct, relays = routes(n)
 
         def rows_of(at):
@@ -160,18 +161,42 @@
             mine = rows_of(me)
             for by in direct:
                 send(mine, mine, s, r.at[by], peer(hand * by))
-            send(mine, mine, s, f_r, f_peer)
+            send(mine, mine, s, f_r.at[0], f_peer)
+            if straight:
+
+                @pl.when(core == 0)
+                def _():
+                    for by in far_first(n):
+                        if by not in direct:
+                            send(mine, mine, s, r.at[by], peer(hand * by))
+
 
         def take(offsets):
             for by in offsets:
                 there = rows_of(lax.rem(me + n * n - hand * by, n))
                 settle(there, r.at[by])
-                for onward in relays.get(by, []):
-                    send(there, there, s, r.at[onward], peer(hand * (onward - by)))
-                send(there, there, s, f_r, f_peer)
+                if by in relays:
+
+                    def onwards():
+                        for onward in relays[by]:
+                            send(there, there, s, r.at[onward], peer(hand * (onward - by)))
+
+                    if straight:
+                        pl.when(core == 1)(onwards)
+                    else:
+                        onwards()
+                send(there, there, s, f_r.at[0 if by in direct else 1], f_peer)
+
+        def rest_near():
+            settle(full.at[pl.ds(0, (1 + len(direct)) * TILE), :], f_r.at[0])
+
+        def rest_far():
+            if len(direct) + 1 < n:
+                settle(full.at[pl.ds(0, (n - 1 - len(direct)) * TILE), :], f_r.at[1])
 
         def rest():
-            settle(full.at[pl.ds(0, half), :], f_r)
+            rest_near()
+            rest_far()
 
         def drained():
             settle(full.at[pl.ds(0, (2 * n - 1) * TILE), :], s)
@@ -179,7 +204,7 @@
         via = [by for by in direct if by in relays]
         near = [by for by in direct if by not in relays]
         far = [by for by in range(1, n) if by not in direct]
-        return first, take, rest, drained, (via, near, sorted(far, key=lambda by: min(by, n - by)))
+        return first, take, (rest, rest_near, rest_far), drained, (via, near, sorted(far, key=lambda by: min(by, n - by)))
 
     def prepared(i, dst, at):
         kept = expanded(codes[i], i < 2, width, height)
@@ -199,19 +224,19 @@
     loads[3].wait()
     prepared(1, wcat, pl.ds(height, height))
 
-    t_first, t_take, t_rest, t_drained, t_at = spread(
+    t_first, t_take, (_, t_rest_near, t_rest_far), t_drained, t_at = spread(
         allt, core * ny, y, ny, y_peer, sent.at[2], ay_r.at[0], ac_r.at[0], core_peer
     )
-    o_first, o_take, o_rest, o_drained, o_at = spread(
+    o_first, o_take, (o_rest, _, _), o_drained, o_at = spread(
         allo, core * ny, y, ny, y_peer, sent.at[3], ay_r.at[1], ac_r.at[1], core_peer
     )
-    for k, (full, first) in enumerate(((allt, t_first), (allo, o_first))):
+    for k, full in enumerate((allt, allo)):
         loads[6 + k].wait()
         if nz > 1:
             settle(zin.at[k, pl.ds(0, nz - 1)], az_r.at[k])
         gathered = jnp.concatenate([zin[k, i].astype(F32) for i in range(nz)], axis=0)
         full[block(core * ny + y), :] = gathered.astype(BF16)
-        first()
+        (t_first, o_first)[k]()
 
     loads[4].wait()
     loads[5].wait()
@@ -220,51 +245,89 @@
     t_take(t_at[0])
     t_take(t_at[1])
     o_take(o_at[0])
+
+    split = width_of[0]
+    parts = ((sum_gu, zl_gu_out, zl_gu_in, x_gu_out, x_gu_in), (sum_b, zl_b_out, zl_b_in, x_b_out, x_b_in))
+
+    def early(offsets):
+        spots = [lax.rem(y + by, ny) for by in offsets]
+        left = jnp.concatenate([allt[block((1 - zl) * ny + at), :] for at in spots], axis=0)
+        product = dot(left, wcat[pl.ds(0, split), :], (1, 1)).astype(BF16)
+        for i, at in enumerate(spots):
+            zl_gu_out[block(at), :] = product[i * TILE : (i + 1) * TILE, :]
+            send(zl_gu_out.at[block(at), :], zl_gu_in.at[block(at), :], sent.at[4], bz_r.at[0, at], zl_peer)
+
+    def late(at):
+        back = dot(allo[at, :], wdown[...], (1, 1))
+        tail = dot(allt[at, :], wcat[pl.ds(split, 2 * height - split), :], (1, 1))
+        return jnp.concatenate([back, tail], axis=1)
+
+    def pair(k, at):
+        total, _, arrived, out, _ = parts[k]
+        there = block(at)
+        settle(arrived.at[there, :], bz_r.at[k, at])
+        out[there, :] = (total[there, :] + arrived[there, :].astype(F32)).astype(BF16)
+
+    def pass_on(k, at, by):
+        out, into = parts[k][3:]
+        send(out.at[block(at), :], into.at[by], sent.at[6 + k], bx_r.at[k], (at * nl + zl, col))
+
+    near = [0] + routes(ny)[0]
+    distant = [by for by in range(1, ny) if by not in near]
+    t_rest_near()
+    early(near)
     t_take(t_at[2])
-    t_rest()
-
-    def owed(total, out, into, k, full, weight):
-        out[...] = dot(full[part(1 - zl), :], weight[...], (1, 1)).astype(BF16)
-        for by in far_first(nx) + [0]:
-            there = block(lax.rem(x + by, nx))
-            send(out.at[there, :], into.at[there, :], sent.at[4 + k], bz_r.at[k, by], zl_peer)
-        total[...] = dot(full[part(zl), :], weight[...], (1, 1))
-
-    owed(sum_gu, zl_gu_out, zl_gu_in, 0, allt, wcat)
+    t_rest_far()
+    if distant:
+        early(distant)
+    sum_gu[...] = dot(allt[part(zl), :], wcat[pl.ds(0, split), :], (1, 1))
+
+    def gu_pairs(offsets):
+        for by in offsets:
+            at = lax.rem(y + by, ny)
+            pair(0, at)
+
+            @pl.when(at != x)
+            def _():
+                pass_on(0, at, lax.rem(at + nx - x, nx))
+
+    gu_pairs(near)
     o_take(o_at[1])
     o_take(o_at[2])
     o_rest()
-    owed(sum_b, zl_b_out, zl_b_in, 1, allo, wdown)
-
-    parts = ((sum_gu, zl_gu_in, x_gu_out, x_gu_in), (sum_b, zl_b_in, x_b_out, x_b_in))
-    for k, (total, arrived, out, into) in enumerate(parts):
-        for by in far_first(nx):
-            there = block(lax.rem(x + by, nx))
-            settle(arrived.at[there, :], bz_r.at[k, by])
-            out[there, :] = (total[there, :] + arrived[there, :].astype(F32)).astype(BF16)
-            send(out.at[there, :], into.at[by], sent.at[6 + k], bx_r.at[k], x_peer(by))
+    zl_b_out[...] = late(part(1 - zl)).astype(BF16)
+    for by in far_first(nx) + [0]:
+        at = lax.rem(x + by, nx)
+        send(zl_b_out.at[block(at), :], zl_b_in.at[block(at), :], sent.at[5], bz_r.at[1, at], zl_peer)
+    sum_b[...] = late(part(zl))
+    gu_pairs(distant)
+    for by in far_first(nx):
+        at = lax.rem(x + by, nx)
+        pair(1, at)
+        pass_on(1, at, by)
+    settle(zl_b_in.at[block(x), :], bz_r.at[1, x])
 
     sums = []
-    for k, (total, arrived, out, into) in enumerate(parts):
+    for k, (total, _, arrived, out, into) in enumerate(parts):
         here = block(x)
-        settle(arrived.at[here, :], bz_r.at[k, 0])
         value = total[here, :] + arrived[here, :].astype(F32)
         settle(into.at[pl.ds(1, nx - 1)], bx_r.at[k])
         for by in range(1, nx):
             value = value + into[by].astype(F32)
         sums.append(value)
 
-    gate, up, back = sums[0][:, :height], sums[0][:, height:], sums[1]
+    gate, back = sums[0][:, :height], sums[1][:, :height]
+    up = jnp.concatenate([sums[0][:, height:], sums[1][:, height:]], axis=1)
     logistic = 1.0 / (1.0 + jnp.exp(-gate))
     swish = gate * logistic
     up_grad = back * swish
     gate_grad = back * up * logistic * (1.0 + gate * (1.0 - logistic))
     mine = block(zl * nx + x)
     gu[mine, :] = jnp.concatenate([gate_grad, up_grad], axis=1).astype(BF16)
-    g_first, g_take, g_rest, g_drained, g_at = spread(
-        gu, zl * nx, x, nx, x_peer, sent.at[8], cx_r.at[0], cz_r.at[0], zl_peer
-    )
-    h_first, h_take, h_rest, h_drained, h_at = spread(
+    g_first, g_take, (g_rest, _, _), g_drained, g_at = spread(
+        gu, zl * nx, x, nx, x_peer, sent.at[8], cx_r.at[0], cz_r.at[0], zl_peer, straight=True
+    )
+    h_first, h_take, (h_rest, _, _), h_drained, h_at = spread(
         hid, zl * nx, x, nx, x_peer, sent.at[9], cx_r.at[1], cz_r.at[1], zl_peer
     )
     g_first()
@@ -273,25 +336,24 @@
     h_first()
     g_take(g_at[1])
     g_take(g_at[2])
-    h_take(h_at[0])
     g_rest()
 
     core_out[...] = dot(gu[part(1 - core), :], wcat[...], (1, 0))
     send(core_out, core_in, sent.at[10], d_r.at[0], core_peer)
     own[...] = dot(gu[part(core), :], wcat[...], (1, 0))
-    h_take(h_at[1])
     settle(core_in, d_r.at[0])
     total = own[...] + core_in[...]
     own[...] = total
     y_out[...] = total.astype(BF16)
     for by in far_first(ny):
         send(y_out.at[block(lax.rem(y + by, ny)), :], y_in.at[by], sent.at[11], d_r.at[1], y_peer(by))
-    h_take(h_at[2])
+    h_take(h_at[0])
+    h_take(h_at[1])
 
     gwg[...] = (dot(gu[:, :height], allt[...], (0, 0)) * keep[pl.ds(0, height), :].astype(F32)).astype(BF16)
     uwg[...] = (dot(gu[:, height:], allt[...], (0, 0)) * keep[pl.ds(height, height), :].astype(F32)).astype(BF16)
-    h_rest()
-
+
+    h_take(h_at[2])
     value = own[block(y), :]
     settle(y_in.at[pl.ds(1, ny - 1)], d_r.at[1])
     for by in range(1, ny):
@@ -301,6 +363,7 @@
     for by in range(1, nz):
         send(z_out.at[lax.rem(z + by, nz)], z_in.at[by], sent.at[12], d_r.at[2], z_peer(by))
 
+    h_rest()
     dwg[...] = (dot(hid[...], allo[...], (0, 0)) * keep[pl.ds(2 * height, height), :].astype(F32)).astype(BF16)
     for k in range(2):
         if nz > 1:
@@ -340,6 +403,8 @@
     rows, width = tokens.shape
     height = down_weight.shape[0]
     half = ny * TILE
+    lead = 2 * height // 128 * 128
+    lag = 3 * height - lead
     dma = pltpu.SemaphoreType.DMA
     vmem = pl.BlockSpec(memory_space=pltpu.VMEM)
     weight = jax.ShapeDtypeStruct((height, width), BF16)
@@ -351,16 +416,16 @@
         pltpu.VMEM((height, width), BF16),
         pltpu.VMEM((3 * height, width), BF16),
         pltpu.VMEM((3, width // 4, height // 4), jnp.int32),
-        pltpu.VMEM((half, 2 * height), BF16),
-        pltpu.VMEM((half, 2 * height), BF16),
-        pltpu.VMEM((half, height), BF16),
-        pltpu.VMEM((half, height), BF16),
-        pltpu.VMEM((half, 2 * height), F32),
-        pltpu.VMEM((half, height), F32),
-        pltpu.VMEM((half, 2 * height), BF16),
-        pltpu.VMEM((nx, TILE, 2 * height), BF16),
-        pltpu.VMEM((half, height), BF16),
-        pltpu.VMEM((nx, TILE, height), BF16),
+        pltpu.VMEM((half, lead), BF16),
+        pltpu.VMEM((half, lead), BF16),
+        pltpu.VMEM((half, lag), BF16),
+        pltpu.VMEM((half, lag), BF16),
+        pltpu.VMEM((half, lead), F32),
+        pltpu.VMEM((half, lag), F32),
+        pltpu.VMEM((half, lead), BF16),
+        pltpu.VMEM((nx, TILE, lead), BF16),
+        pltpu.VMEM((half, lag), BF16),
+        pltpu.VMEM((nx, TILE, lag), BF16),
         pltpu.VMEM((2 * half, 2 * height), BF16),
         pltpu.VMEM((2 * half, height), BF16),
         pltpu.VMEM((half, width), F32),
@@ -370,8 +435,8 @@
         pltpu.VMEM((ny, TILE, width), BF16),
         pltpu.VMEM((nz, rows, width), F32),
         pltpu.VMEM((nz, rows, width), F32),
-        dma((8,)), dma((13,)), dma((2,)), dma((2, ny)), dma((2,)),
-        dma((2, nx)), dma((2,)), dma((2, nx)), dma((2,)), dma((3,)),
+        dma((8,)), dma((13,)), dma((2,)), dma((2, ny)), dma((2, 2)),
+        dma((2, nx)), dma((2,)), dma((2, nx)), dma((2, 2)), dma((3,)),
     ]
     held = (jax.ShapeDtypeStruct((rows, width), BF16), weight, weight, weight)
     results = pl.pallas_call(

time: 73.5 us -> 73 us (level)
  no operation moved by 1% of the time
where the time goes in v3:
time: 73 us; the launch traced here: 72.8 us
  Pallas kernels  72.2 us (99%)
    pallas_call x1, Pallas kernels, local(): pl.pallas_call(functools.partial(kernel, dims), out_shape=held, in_specs=...  71 us

profile of v3, /device:TPU:1, one launch (start us, length us, event | category | flops | bytes accessed | tf_op | source)
XLA Modules:
  0.0 72.8 jit_solution(3877356776828949351)
XLA Ops:
  0.6 71.0 %block.1 = (bf16[4,640]{1,0:T(4,128)(2,1)S(1)}, bf16[416,640]{1,0:T(8,128)(2,1)S(1)}, bf16[416,640]{1,0:T(8,128)(2,1)S(1)}, bf16[416,640]{1,0:T(8,128)(2,1)S(1)}) custom-call(bf16[4,640]{1,0:T(4,128)(2,1)} %tok.1, bf16[4,640]{1,0:T(4,128)(2,1)} %og.1, bf16[416,640]{1,0:T(8,128)(2,1)} %bitcast.5, bf16[416,640]{1,0:T(8,128)(2,1)} %bitcast.6, ...), custom_call_target="tpu_custom_call" | custom-call | tf_op jit(solution)/shard_map/block/pallas_call | solution.py:442
  71.6 1.2 %write.1 = (bf16[4,640]{1,0:T(4,128)(2,1)}, bf16[416,640]{1,0:T(8,128)(2,1)}, bf16[416,640]{1,0:T(8,128)(2,1)}, bf16[416,640]{1,0:T(8,128)(2,1)}) custom-call(bf16[4,640]{1,0:T(4,128)(2,1)S(1)} %get-tuple-element.12.refs_0_, bf16[416,640]{1,0:T(8,128)(2,1)S(1)} %get-tuple-element.13.refs_1_, bf16[416,640]{1,0:T(8,128)(2,1)S(1)} %get-tuple-element.14.refs_2_, ...), custom_call_target="tpu_custom_call" | custom-call | tf_op jit(solution)/shard_map/write/pallas_call | solution.py:461

commit v4 on v3

--- a/solution.py
+++ b/solution.py
@@ -227,7 +227,7 @@
     t_first, t_take, (_, t_rest_near, t_rest_far), t_drained, t_at = spread(
         allt, core * ny, y, ny, y_peer, sent.at[2], ay_r.at[0], ac_r.at[0], core_peer
     )
-    o_first, o_take, (o_rest, _, _), o_drained, o_at = spread(
+    o_first, o_take, (_, o_rest_near, o_rest_far), o_drained, o_at = spread(
         allo, core * ny, y, ny, y_peer, sent.at[3], ay_r.at[1], ac_r.at[1], core_peer
     )
     for k, full in enumerate((allt, allo)):
@@ -249,18 +249,22 @@
     split = width_of[0]
     parts = ((sum_gu, zl_gu_out, zl_gu_in, x_gu_out, x_gu_in), (sum_b, zl_b_out, zl_b_in, x_b_out, x_b_in))
 
-    def early(offsets):
+    def product(k, rows_in):
+        if k == 0:
+            return dot(rows_in(allt), wcat[pl.ds(0, split), :], (1, 1))
+        back = dot(rows_in(allo), wdown[...], (1, 1))
+        tail = dot(rows_in(allt), wcat[pl.ds(split, 2 * height - split), :], (1, 1))
+        return jnp.concatenate([back, tail], axis=1)
+
+    def early(k, offsets):
+        out, arriving = parts[k][1:3]
         spots = [lax.rem(y + by, ny) for by in offsets]
-        left = jnp.concatenate([allt[block((1 - zl) * ny + at), :] for at in spots], axis=0)
-        product = dot(left, wcat[pl.ds(0, split), :], (1, 1)).astype(BF16)
+        formed = product(
+            k, lambda full: jnp.concatenate([full[block((1 - zl) * ny + at), :] for at in spots], axis=0)
+        ).astype(BF16)
         for i, at in enumerate(spots):
-            zl_gu_out[block(at), :] = product[i * TILE : (i + 1) * TILE, :]
-            send(zl_gu_out.at[block(at), :], zl_gu_in.at[block(at), :], sent.at[4], bz_r.at[0, at], zl_peer)
-
-    def late(at):
-        back = dot(allo[at, :], wdown[...], (1, 1))
-        tail = dot(allt[at, :], wcat[pl.ds(split, 2 * height - split), :], (1, 1))
-        return jnp.concatenate([back, tail], axis=1)
+            out[block(at), :] = formed[i * TILE : (i + 1) * TILE, :]
+            send(out.at[block(at), :], arriving.at[block(at), :], sent.at[4 + k], bz_r.at[k, at], zl_peer)
 
     def pair(k, at):
         total, _, arrived, out, _ = parts[k]
@@ -275,37 +279,34 @@
     near = [0] + routes(ny)[0]
     distant = [by for by in range(1, ny) if by not in near]
     t_rest_near()
-    early(near)
+    early(0, near)
     t_take(t_at[2])
     t_rest_far()
     if distant:
-        early(distant)
-    sum_gu[...] = dot(allt[part(zl), :], wcat[pl.ds(0, split), :], (1, 1))
-
-    def gu_pairs(offsets):
+        early(0, distant)
+    sum_gu[...] = product(0, lambda full: full[part(zl), :])
+
+    def pairs(k, offsets):
         for by in offsets:
             at = lax.rem(y + by, ny)
-            pair(0, at)
+            pair(k, at)
 
             @pl.when(at != x)
             def _():
-                pass_on(0, at, lax.rem(at + nx - x, nx))
-
-    gu_pairs(near)
+                pass_on(k, at, lax.rem(at + nx - x, nx))
+
+    pairs(0, near)
     o_take(o_at[1])
+    o_rest_near()
+    early(1, near)
     o_take(o_at[2])
-    o_rest()
-    zl_b_out[...] = late(part(1 - zl)).astype(BF16)
-    for by in far_first(nx) + [0]:
-        at = lax.rem(x + by, nx)
-        send(zl_b_out.at[block(at), :], zl_b_in.at[block(at), :], sent.at[5], bz_r.at[1, at], zl_peer)
-    sum_b[...] = late(part(zl))
-    gu_pairs(distant)
-    for by in far_first(nx):
-        at = lax.rem(x + by, nx)
-        pair(1, at)
-        pass_on(1, at, by)
-    settle(zl_b_in.at[block(x), :], bz_r.at[1, x])
+    o_rest_far()
+    if distant:
+        early(1, distant)
+    sum_b[...] = product(1, lambda full: full[part(zl), :])
+    pairs(0, distant)
+    pairs(1, near)
+    pairs(1, distant)
 
     sums = []
     for k, (total, _, arrived, out, into) in enumerate(parts):

time: 73 us -> 73.8 us (1.011)
  Pallas kernels: 72.2 us -> 73 us
    pallas_call x1, Pallas kernels: 71 us -> 71.8 us  [local(): pl.pallas_call(functools.partial(kernel, dims), out_shape=held, in_specs=...]
where the time goes in v4:
time: 73.8 us; the launch traced here: 73.6 us
  Pallas kernels  73 us (99%)
    pallas_call x1, Pallas kernels, local(): pl.pallas_call(functools.partial(kernel, dims), out_shape=held, in_specs=...  71.8 us

profile of v4, /device:TPU:1, one launch (start us, length us, event | category | flops | bytes accessed | tf_op | source)
XLA Modules:
  0.0 73.6 jit_solution(17713751722609841873)
XLA Ops:
  0.6 71.8 %block.1 = (bf16[4,640]{1,0:T(4,128)(2,1)S(1)}, bf16[416,640]{1,0:T(8,128)(2,1)S(1)}, bf16[416,640]{1,0:T(8,128)(2,1)S(1)}, bf16[416,640]{1,0:T(8,128)(2,1)S(1)}) custom-call(bf16[4,640]{1,0:T(4,128)(2,1)} %tok.1, bf16[4,640]{1,0:T(4,128)(2,1)} %og.1, bf16[416,640]{1,0:T(8,128)(2,1)} %bitcast.5, bf16[416,640]{1,0:T(8,128)(2,1)} %bitcast.6, ...), custom_call_target="tpu_custom_call" | custom-call | tf_op jit(solution)/shard_map/block/pallas_call | solution.py:443
  72.5 1.2 %write.1 = (bf16[4,640]{1,0:T(4,128)(2,1)}, bf16[416,640]{1,0:T(8,128)(2,1)}, bf16[416,640]{1,0:T(8,128)(2,1)}, bf16[416,640]{1,0:T(8,128)(2,1)}) custom-call(bf16[4,640]{1,0:T(4,128)(2,1)S(1)} %get-tuple-element.12.refs_0_, bf16[416,640]{1,0:T(8,128)(2,1)S(1)} %get-tuple-element.13.refs_1_, bf16[416,640]{1,0:T(8,128)(2,1)S(1)} %get-tuple-element.14.refs_2_, ...), custom_call_target="tpu_custom_call" | custom-call | tf_op jit(solution)/shard_map/write/pallas_call | solution.py:462
